TPU v7x, 32 devices: a whole 2x2x4 slice. The times are simulated.
32 devices in a mesh: gx: 4 (over y, core), gy: 8 (over z, x).
Axes of the slice: x: 2, y: 2, z: 4, core: 2. Of those that a mesh axis runs over, the one named last changes fastest.
Arguments:
- a_rows: bfloat16 [196608, 1024], P(('gx', 'gy')), may hold values from -6 to 6
- heights: int32 [32], P('gx'), may hold values from 1 to 38, as said below
- destination: int32 [32, 48], P('gx'), may hold values from 0 to 1023, as said below
Outputs:
- ortho_rows: bfloat16 [131072, 1024], P(('gx', 'gy'))
- factor_r: float32 [1024, 1024], replicated
Inputs may be any that keep to these rules, and one draw needn't show every extreme that they name: Tiles 0 to heights[d] - 1 of device d are live, the others carry nothing of the problem; the largest value is reached in every draw. For a live tile, destination // 32 is a device with the same gx index as the tile's device; live tiles name distinct slots; one device sends at most one live tile to any other device; entries of tiles that are not live are meaningless.
All inputs are finite; a program needn't handle non-finite values.
Results may differ from a plain program's by a relative error of at most 0.00055.
Values may be sent and summed in bfloat16 or wider, within the bound.
A program may use at most 256 MiB of HBM per device.

v0:
```python
import math
import jax
import jax.numpy as jnp
from jax import lax
from jax.sharding import PartitionSpec as P

TILE = 128
SLOTS = 32


def factor(row_block):
    gram_local = lax.dot_general(
        row_block, row_block, (((0,), (0,)), ((), ())), preferred_element_type=jnp.float32
    )
    summed = lax.psum(gram_local, ("gx", "gy"))
    return jnp.linalg.cholesky(summed)


def normalise(low_factor, row_block, root_scale):
    solved = jax.scipy.linalg.solve_triangular(
        low_factor, row_block.astype(jnp.float32).T, lower=True
    )
    return (solved.T * root_scale).astype(jnp.bfloat16)


def on_device(a_rows, heights, destination):
    breadth = a_rows.shape[1]
    size_gy = lax.axis_size("gy")
    devices = lax.axis_size("gx") * size_gy
    group_pos = lax.axis_index("gy")
    my_index = lax.axis_index("gx") * size_gy + group_pos
    group_base = my_index - group_pos
    tile_stack = a_rows.reshape(-1, TILE, breadth)
    stored = tile_stack.shape[0]
    tile_ids = jnp.arange(stored, dtype=jnp.int32)
    peer_ids = jnp.arange(size_gy, dtype=jnp.int32)
    slot_ids = jnp.arange(SLOTS, dtype=jnp.int32)
    tile_live = tile_ids[None, :] < heights[:, None]
    target_dev = destination // SLOTS
    target_slot = destination % SLOTS
    own_live = tile_live[group_pos]
    own_dev = target_dev[group_pos]
    own_slot = target_slot[group_pos]
    leaving = own_live & (own_dev != my_index)
    chosen = leaving[None, :] & (own_dev[None, :] - group_base == peer_ids[:, None])
    send_index = jnp.sum(jnp.where(chosen, tile_ids[None, :], 0), axis=1)
    send_has = jnp.any(chosen, axis=1)
    arriving = tile_live & (target_dev == my_index) & (peer_ids[:, None] != group_pos)
    arrive_slot = jnp.sum(jnp.where(arriving, target_slot, 0), axis=1)
    arrive_has = jnp.any(arriving, axis=1)
    staying = own_live & (own_dev == my_index)
    own_match = staying[None, :] & (own_slot[None, :] == slot_ids[:, None])
    in_match = arrive_has[None, :] & (arrive_slot[None, :] == slot_ids[:, None])
    matched = jnp.concatenate([own_match, in_match], axis=1)
    source = jnp.sum(
        jnp.where(matched, jnp.arange(stored + size_gy, dtype=jnp.int32)[None, :], 0), axis=1
    )
    filled = jnp.any(matched, axis=1)
    root_scale = math.sqrt(devices * SLOTS * TILE)
    received = lax.all_to_all(
        jnp.where(send_has[:, None, None], tile_stack[send_index], jnp.zeros((), tile_stack.dtype)),
        "gy",
        split_axis=0,
        concat_axis=0,
        tiled=True,
    )
    combined = jnp.concatenate([tile_stack, received], axis=0)
    balanced = jnp.where(
        filled[:, None, None], combined[source], jnp.zeros((), tile_stack.dtype)
    ).reshape(-1, breadth)
    low_factor = factor(balanced)
    ortho_rows = normalise(low_factor, balanced, root_scale)
    return (ortho_rows, low_factor.T / root_scale)


def solution(mesh):
    placed = (P(("gx", "gy"), None), P("gx"), P("gx", None))
    return jax.shard_map(
        on_device,
        mesh=mesh,
        in_specs=placed,
        out_specs=(P(("gx", "gy"), None), P()),
        check_vma=False,
    )
```

profile of v0, /device:TPU:0, one launch (start us, length us, event | category | flops | bytes accessed | tf_op | source)
XLA Modules:
  0.0 704.4 jit_solution(5128577823372429109)
XLA Ops:
  23.8 47.7 %all-to-all-done = bf16[8,128,1024]{2,1,0:T(8,128)(2,1)S(1)} async-done(((bf16[8,128,1024]{2,1,0:T(8,128)(2,1)}), bf16[8,128,1024]{2,1,0:T(8,128)(2,1)S(1)}, u32[]{:S(2)}, u32[]{:S(2)}) %all-to-all-start) | async-done | bytes 2097184 | tf_op jit(solution)/shard_map/all_to_all | solution.py:60
  71.5 13.6 %pad_maximum_fusion = bf16[56,128,1024]{2,1,0:T(8,128)(2,1)} fusion(bf16[8,128,1024]{2,1,0:T(8,128)(2,1)S(1)} %all-to-all-done, bf16[48,128,1024]{2,1,0:T(8,128)(2,1)} %bitcast.134), kind=kLoop, calls=%fused_computation.5 | loop fusion | flops 7340032 | bytes 29360128 | tf_op jit(solution)/shard_map/concatenate | solution.py:67
  85.1 10.4 %gather_fusion.1 = bf16[32,128,1024]{2,1,0:T(8,128)(2,1)} fusion(bf16[56,128,1024]{2,1,0:T(8,128)(2,1)} %pad_maximum_fusion, s32[1024]{0:T(1024)S(1)} %pad_clamp_fusion), kind=kCustom, calls=%fused_computation.1 | custom fusion | bytes 16777344 | tf_op jit(solution)/shard_map/gather | solution.py:69
  95.4 15.6 %fusion.30 = f32[1024,1024]{0,1:T(8,128)} fusion(bf16[32,128,1024]{2,1,0:T(8,128)(2,1)} %gather_fusion.1, pred[32]{0:T(512)(128)(4,1)S(1)} %reduce_or.41), kind=kOutput, calls=%fused_computation.43 | convolution fusion | flops 8594128896 | bytes 12582944 | tf_op jit(solution)/shard_map/dot_general | solution.py:12
  111.2 11.6 %copy.26 = bf16[4096,1024]{0,1:T(8,128)(2,1)} copy(bf16[4096,1024]{1,0:T(8,128)(2,1)} %bitcast.132) | data formatting | bytes 16777216 | tf_op jit(solution)/shard_map/gather | solution.py:69
  122.7 11.5 %fusion.90 = (f32[1024,4096]{1,0:T(8,128)}, bf16[1024,4096]{1,0:T(8,128)(2,1)}) fusion(bf16[4096,1024]{0,1:T(8,128)(2,1)} %copy.26, pred[4096]{0:T(1024)(128)(4,1)S(1)} %broadcast_bitcast_fusion), kind=kLoop, calls=%fused_computation.208 | loop fusion | flops 8388608 | bytes 33558528 | tf_op jit(solution)/shard_map/transpose | solution.py:21
  134.3 118.5 %all-reduce.3.cloned.1.call-done = f32[1024,1024]{0,1:T(8,128)} async-done(((f32[1024,1024]{0,1:T(8,128)}), f32[1024,1024]{0,1:T(8,128)}) %all-reduce.3.cloned.1.call-update) | async-done | bytes 4194320 | tf_op jit(solution)/shard_map/psum | solution.py:15
  264.7 11.7 %cholesky.223 = f32[128,128]{1,0:T(8,128)S(1)} custom-call(f32[128,128]{1,0:T(8,128)S(1)} %cholesky.580), custom_call_target="Cholesky" | custom-call | tf_op jit(solution)/shard_map/jit(cholesky)/cholesky | solution.py:16
  293.4 12.2 %cholesky.244 = f32[128,128]{1,0:T(8,128)S(1)} custom-call(f32[128,128]{1,0:T(8,128)S(1)} %cholesky.584), custom_call_target="Cholesky" | custom-call | tf_op jit(solution)/shard_map/jit(cholesky)/cholesky | solution.py:16
  306.9 9.8 %custom-call.64 = f32[1,128,128]{1,2,0:T(8,128)S(1)} custom-call(f32[1,128,128]{2,1,0:T(8,128)S(1)} %get-tuple-element.80), custom_call_target="InvertDiagBlocksLowerTriangular" | custom-call | tf_op jit(solution)/shard_map/jit(cholesky)/cholesky | solution.py:16
  320.0 11.7 %cholesky.468 = f32[128,128]{1,0:T(8,128)S(1)} custom-call(f32[128,128]{1,0:T(8,128)S(1)} %cholesky.589), custom_call_target="Cholesky" | custom-call | tf_op jit(solution)/shard_map/jit(cholesky)/cholesky | solution.py:16
  346.3 11.8 %cholesky.487 = f32[128,128]{1,0:T(8,128)S(1)} custom-call(f32[128,128]{1,0:T(8,128)S(1)} %cholesky.594), custom_call_target="Cholesky" | custom-call | tf_op jit(solution)/shard_map/jit(cholesky)/cholesky | solution.py:16
  372.7 11.7 %cholesky.506 = f32[128,128]{1,0:T(8,128)S(1)} custom-call(f32[128,128]{1,0:T(8,128)S(1)} %cholesky.599), custom_call_target="Cholesky" | custom-call | tf_op jit(solution)/shard_map/jit(cholesky)/cholesky | solution.py:16
  385.8 10.0 %custom-call.67 = f32[1,128,128]{1,2,0:T(8,128)S(1)} custom-call(f32[1,128,128]{2,1,0:T(8,128)S(1)} %get-tuple-element.71), custom_call_target="InvertDiagBlocksLowerTriangular" | custom-call | tf_op jit(solution)/shard_map/jit(cholesky)/cholesky | solution.py:16
  399.0 11.7 %cholesky.526 = f32[128,128]{1,0:T(8,128)S(1)} custom-call(f32[128,128]{1,0:T(8,128)S(1)} %cholesky.604), custom_call_target="Cholesky" | custom-call | tf_op jit(solution)/shard_map/jit(cholesky)/cholesky | solution.py:16
  412.0 9.8 %custom-call.68 = f32[1,128,128]{1,2,0:T(8,128)S(1)} custom-call(f32[1,128,128]{2,1,0:T(8,128)S(1)} %get-tuple-element.68), custom_call_target="InvertDiagBlocksLowerTriangular" | custom-call | tf_op jit(solution)/shard_map/jit(cholesky)/cholesky | solution.py:16
  424.8 12.1 %cholesky.546 = f32[128,128]{1,0:T(8,128)S(1)} custom-call(f32[128,128]{1,0:T(8,128)S(1)} %cholesky.609), custom_call_target="Cholesky" | custom-call | tf_op jit(solution)/shard_map/jit(cholesky)/cholesky | solution.py:16
  438.2 9.8 %custom-call.69 = f32[1,128,128]{1,2,0:T(8,128)S(1)} custom-call(f32[1,128,128]{2,1,0:T(8,128)S(1)} %get-tuple-element.65), custom_call_target="InvertDiagBlocksLowerTriangular" | custom-call | tf_op jit(solution)/shard_map/jit(cholesky)/cholesky | solution.py:16
  450.7 11.7 %cholesky.564 = f32[128,128]{1,0:T(8,128)S(1)} custom-call(f32[128,128]{1,0:T(8,128)S(1)} %convolution_subtract_fusion.11), custom_call_target="Cholesky" | custom-call | tf_op jit(solution)/shard_map/jit(cholesky)/cholesky | solution.py:16
  480.7 23.4 %while.1 = (s32[]{:T(128)}, f32[1024,1024]{1,0:T(8,128)}, s32[8,2]{0,1:T(2,128)S(1)}, f32[8,128,128]{2,1,0:T(8,128)S(1)}, s32[]{:T(128)}) while((s32[]{:T(128)}, f32[1024,1024]{1,0:T(8,128)}, s32[8,2]{0,1:T(2,128)S(1)}, f32[8,128,128]{2,1,0:T(8,128)S(1)}, s32[]{:T(128)}) %tuple.74), condition=%wide.while_cond, body=%wide.while_body.sunk | while | flops 2 | bytes 131189 | solution.py:20
  504.1 78.8 %custom-call.70 = f32[8,128,128]{1,2,0:T(8,128)S(1)} custom-call(f32[8,128,128]{2,1,0:T(8,128)S(1)} %get-tuple-element.9), custom_call_target="InvertDiagBlocksLowerTriangular" | custom-call | tf_op jit(solution)/shard_map/jit(_solve_triangular)/triangular_solve | solution.py:20
  645.8 9.8 %convolution_subtract_fusion = f32[128,4096]{1,0:T(8,128)S(1)} fusion(f32[768,4096]{1,0:T(8,128)} %get-tuple-element.41, f32[1024,4096]{1,0:T(8,128)S(1)} %bitcast.131, f32[1024,1024]{1,0:T(8,128)} %get-tuple-element.145), kind=kOutput, calls=%fused_computation.26 | convolution fusion | flops 4832362496 | bytes 17170432 | tf_op jit(solution)/shard_map/jit(_solve_triangular)/triangular_solve | solution.py:20
  660.4 11.7 %convolution_subtract_fusion.4 = f32[128,4096]{1,0:T(8,128)S(1)} fusion(f32[896,4096]{1,0:T(8,128)} %get-tuple-element.37, f32[1024,4096]{1,0:T(8,128)S(1)} %bitcast.131, f32[1024,1024]{1,0:T(8,128)} %get-tuple-element.145), kind=kOutput, calls=%fused_computation.30 | convolution fusion | flops 5637668864 | bytes 19333120 | tf_op jit(solution)/shard_map/jit(_solve_triangular)/triangular_solve | solution.py:20
  685.4 11.9 %copy.27 = bf16[4096,1024]{1,0:T(8,128)(2,1)} copy(bf16[4096,1024]{0,1:T(8,128)(2,1)} %fusion) | data formatting | bytes 16777216
  (121 shorter events, 209.6 us)
Async XLA Ops:
  16.0 55.5 %all-to-all-start = ((bf16[8,128,1024]{2,1,0:T(8,128)(2,1)}), bf16[8,128,1024]{2,1,0:T(8,128)(2,1)S(1)}, u32[]{:S(2)}, u32[]{:S(2)}) async-start(bf16[8,128,1024]{2,1,0:T(8,128)(2,1)} %broadcast_select_fusion), calls=%async_computation | async-start | bytes 4194304 | tf_op jit(solution)/shard_map/all_to_all | solution.py:60
  23.3 229.5 %all-reduce.3.cloned.1.call-start = ((), (), s32[]{:S(2)}) async-start(), calls=%async_computation.1 | async-start | bytes 8388608 | tf_op jit(solution)/shard_map/psum | solution.py:15
  262.8 1.9 copy-start
  582.9 29.7 %copy-start.1 = (f32[8,128,128]{1,2,0:T(8,128)}, f32[8,128,128]{1,2,0:T(8,128)S(1)}, u32[]{:S(2)}) copy-start(f32[8,128,128]{1,2,0:T(8,128)S(1)} %custom-call.70) | copy-start | bytes 1572868
  582.9 15.6 %slice-start = ((s8[16777216]{0:T(1024)(128)(4,1)}), s8[4194304]{0:T(1024)(128)(4,1)S(1)}, s32[]{:S(2)}) async-start(s8[16777216]{0:T(1024)(128)(4,1)} %bitcast.130), calls=%async_computation.2 | async-start | bytes 8388608
  582.9 15.6 %slice-start.1 = ((s8[16777216]{0:T(1024)(128)(4,1)}), s8[4194304]{0:T(1024)(128)(4,1)S(1)}, s32[]{:S(2)}) async-start(s8[16777216]{0:T(1024)(128)(4,1)} %bitcast.130), calls=%async_computation.3 | async-start | bytes 8388608
  589.0 9.5 %slice-start.2 = ((s8[16777216]{0:T(1024)(128)(4,1)}), s8[4194304]{0:T(1024)(128)(4,1)S(1)}, s32[]{:S(2)}) async-start(s8[16777216]{0:T(1024)(128)(4,1)} %bitcast.130), calls=%async_computation.4 | async-start | bytes 8388608
  592.8 5.8 slice-start.3
Sparse Core Ops, SparseCore 0:
  111.2 141.4 all-reduce.2
where the time goes:
time: 712 us; the launch traced here: 704 us
  other arithmetic  301 us (42%)
  waiting for transfers between devices  166 us (23%)
  matrix products  132 us (19%)
  local copies, waits for them, and re-layouts  78 us (11%)
  between operations  19.5 us (3%)
  starting transfers between devices  7.32 us (1%)
    another operation x31, other arithmetic, factor(): return jnp.linalg.cholesky(summed)  173 us
    psum x1, waiting for transfers between devices, factor(): summed = lax.psum(gram_local, ('gx', 'gy'))  118 us
    another operation x15, matrix products, normalise(): jax.scipy.linalg.solve_triangular(low_factor, row_block.astype(jnp.float3...  93.2 us
    another operation x2, other arithmetic, normalise(): jax.scipy.linalg.solve_triangular(low_factor, row_block.astype(jnp.float3...  78.8 us
    all_to_all x1, waiting for transfers between devices, on_device(): lax.all_to_all(jnp.where(send_has[:, None, None], tile_stack[send_index],...  47.7 us
    another operation x24, local copies, waits for them, and re-layouts  23.3 us
    another operation x14, matrix products, factor(): return jnp.linalg.cholesky(summed)  23 us
    gather x2, local copies, waits for them, and re-layouts, on_device(): combined[source]  21.9 us
  transfers between devices with their start and end apart: 2, of which 2 were waited for; matrix products, arithmetic and copies ran while one was open for 3% of the time, Pallas kernels for 0%

commit v1 on v0

--- a/solution.py
+++ b/solution.py
@@ -9,10 +9,16 @@
 
 
 def factor(row_block):
+
+    def raise_cards(local_array, named_axis, mesh_name):
+        for ix in (named_axis, mesh_name):
+            local_array = lax.psum(local_array, ix)
+        return local_array
+
     gram_local = lax.dot_general(
         row_block, row_block, (((0,), (0,)), ((), ())), preferred_element_type=jnp.float32
     )
-    summed = lax.psum(gram_local, ("gx", "gy"))
+    summed = raise_cards(gram_local, "gy", "gx")
     return jnp.linalg.cholesky(summed)
 
 

time: 712 us -> 813 us (1.14)
  waiting for transfers between devices: 166 us -> 267 us
    psum x1 -> x2, waiting for transfers between devices: 118 us -> 219 us  [raise_cards(): local_array = lax.psum(local_array, ix)]
  transfers between devices with their start and end apart: 2 -> 3, of which waited for: 2 -> 3; matrix products, arithmetic and copies ran while one was open for 3% -> 3% of each run, Pallas kernels for 0% -> 0%
where the time goes in v1:
time: 813 us; the launch traced here: 805 us
  other arithmetic  301 us (37%)
  waiting for transfers between devices  267 us (33%)
  matrix products  132 us (16%)
  local copies, waits for them, and re-layouts  77.8 us (10%)
  between operations  19.5 us (2%)
    psum x2, waiting for transfers between devices, raise_cards(): local_array = lax.psum(local_array, ix)  219 us
    another operation x31, other arithmetic, factor(): return jnp.linalg.cholesky(summed)  173 us
    another operation x15, matrix products, normalise(): jax.scipy.linalg.solve_triangular(low_factor, row_block.astype(jnp.float3...  93.2 us
    another operation x2, other arithmetic, normalise(): jax.scipy.linalg.solve_triangular(low_factor, row_block.astype(jnp.float3...  78.8 us
    all_to_all x1, waiting for transfers between devices, on_device(): lax.all_to_all(jnp.where(send_has[:, None, None], tile_stack[send_index],...  47.7 us
    another operation x24, local copies, waits for them, and re-layouts  23.3 us
    another operation x14, matrix products, factor(): return jnp.linalg.cholesky(summed)  23 us
    gather x2, local copies, waits for them, and re-layouts, on_device(): combined[source]  21.7 us
  transfers between devices with their start and end apart: 3, of which 3 were waited for; matrix products, arithmetic and copies ran while one was open for 3% of the time, Pallas kernels for 0%

profile of v1, /device:TPU:0, one launch (start us, length us, event | category | flops | bytes accessed | tf_op | source)
XLA Modules:
  0.0 805.1 jit_solution(15092592858500640551)
XLA Ops:
  23.8 47.7 %all-to-all-done = bf16[8,128,1024]{2,1,0:T(8,128)(2,1)S(1)} async-done(((bf16[8,128,1024]{2,1,0:T(8,128)(2,1)}), bf16[8,128,1024]{2,1,0:T(8,128)(2,1)S(1)}, u32[]{:S(2)}, u32[]{:S(2)}) %all-to-all-start) | async-done | bytes 2097184 | tf_op jit(solution)/shard_map/all_to_all | solution.py:66
  71.5 13.6 %pad_maximum_fusion = bf16[56,128,1024]{2,1,0:T(8,128)(2,1)} fusion(bf16[8,128,1024]{2,1,0:T(8,128)(2,1)S(1)} %all-to-all-done, bf16[48,128,1024]{2,1,0:T(8,128)(2,1)} %bitcast.134), kind=kLoop, calls=%fused_computation.5 | loop fusion | flops 7340032 | bytes 29360128 | tf_op jit(solution)/shard_map/concatenate | solution.py:73
  85.1 10.4 %gather_fusion.1 = bf16[32,128,1024]{2,1,0:T(8,128)(2,1)} fusion(bf16[56,128,1024]{2,1,0:T(8,128)(2,1)} %pad_maximum_fusion, s32[1024]{0:T(1024)S(1)} %pad_clamp_fusion), kind=kCustom, calls=%fused_computation.1 | custom fusion | bytes 16777344 | tf_op jit(solution)/shard_map/gather | solution.py:75
  95.4 15.6 %fusion.30 = f32[1024,1024]{0,1:T(8,128)} fusion(bf16[32,128,1024]{2,1,0:T(8,128)(2,1)} %gather_fusion.1, pred[32]{0:T(512)(128)(4,1)S(1)} %reduce_or.41), kind=kOutput, calls=%fused_computation.43 | convolution fusion | flops 8594128896 | bytes 12582944 | tf_op jit(solution)/shard_map/dot_general | solution.py:18
  111.1 155.5 %all-reduce.4.cloned.1.call-done = f32[1024,1024]{0,1:T(8,128)} async-done(((f32[1024,1024]{0,1:T(8,128)}), f32[1024,1024]{0,1:T(8,128)}) %all-reduce.4.cloned.1.call-update) | async-done | bytes 4194320 | tf_op jit(solution)/shard_map/psum | solution.py:15
  266.7 11.3 %copy.26 = bf16[4096,1024]{0,1:T(8,128)(2,1)} copy(bf16[4096,1024]{1,0:T(8,128)(2,1)} %bitcast.132) | data formatting | bytes 16777216 | tf_op jit(solution)/shard_map/gather | solution.py:75
  278.0 11.5 %fusion.90 = (f32[1024,4096]{1,0:T(8,128)}, bf16[1024,4096]{1,0:T(8,128)(2,1)}) fusion(bf16[4096,1024]{0,1:T(8,128)(2,1)} %copy.26, pred[4096]{0:T(1024)(128)(4,1)S(1)} %broadcast_bitcast_fusion), kind=kLoop, calls=%fused_computation.208 | loop fusion | flops 8388608 | bytes 33558528 | tf_op jit(solution)/shard_map/transpose | solution.py:27
  289.6 63.9 %all-reduce.6.cloned.1.call-done = f32[1024,1024]{0,1:T(8,128)} async-done(((f32[1024,1024]{0,1:T(8,128)}), f32[1024,1024]{0,1:T(8,128)}) %all-reduce.6.cloned.1.call-update) | async-done | bytes 4194320 | tf_op jit(solution)/shard_map/psum | solution.py:15
  365.5 11.7 %cholesky.223 = f32[128,128]{1,0:T(8,128)S(1)} custom-call(f32[128,128]{1,0:T(8,128)S(1)} %cholesky.580), custom_call_target="Cholesky" | custom-call | tf_op jit(solution)/shard_map/jit(cholesky)/cholesky | solution.py:22
  394.1 12.2 %cholesky.244 = f32[128,128]{1,0:T(8,128)S(1)} custom-call(f32[128,128]{1,0:T(8,128)S(1)} %cholesky.584), custom_call_target="Cholesky" | custom-call | tf_op jit(solution)/shard_map/jit(cholesky)/cholesky | solution.py:22
  407.6 9.8 %custom-call.64 = f32[1,128,128]{1,2,0:T(8,128)S(1)} custom-call(f32[1,128,128]{2,1,0:T(8,128)S(1)} %get-tuple-element.80), custom_call_target="InvertDiagBlocksLowerTriangular" | custom-call | tf_op jit(solution)/shard_map/jit(cholesky)/cholesky | solution.py:22
  420.7 11.7 %cholesky.468 = f32[128,128]{1,0:T(8,128)S(1)} custom-call(f32[128,128]{1,0:T(8,128)S(1)} %cholesky.589), custom_call_target="Cholesky" | custom-call | tf_op jit(solution)/shard_map/jit(cholesky)/cholesky | solution.py:22
  433.7 9.8 %custom-call.65 = f32[1,128,128]{1,2,0:T(8,128)S(1)} custom-call(f32[1,128,128]{2,1,0:T(8,128)S(1)} %get-tuple-element.77), custom_call_target="InvertDiagBlocksLowerTriangular" | custom-call | tf_op jit(solution)/shard_map/jit(cholesky)/cholesky | solution.py:22
  447.0 11.8 %cholesky.487 = f32[128,128]{1,0:T(8,128)S(1)} custom-call(f32[128,128]{1,0:T(8,128)S(1)} %cholesky.594), custom_call_target="Cholesky" | custom-call | tf_op jit(solution)/shard_map/jit(cholesky)/cholesky | solution.py:22
  473.5 11.7 %cholesky.506 = f32[128,128]{1,0:T(8,128)S(1)} custom-call(f32[128,128]{1,0:T(8,128)S(1)} %cholesky.599), custom_call_target="Cholesky" | custom-call | tf_op jit(solution)/shard_map/jit(cholesky)/cholesky | solution.py:22
  486.5 10.0 %custom-call.67 = f32[1,128,128]{1,2,0:T(8,128)S(1)} custom-call(f32[1,128,128]{2,1,0:T(8,128)S(1)} %get-tuple-element.71), custom_call_target="InvertDiagBlocksLowerTriangular" | custom-call | tf_op jit(solution)/shard_map/jit(cholesky)/cholesky | solution.py:22
  499.8 11.7 %cholesky.526 = f32[128,128]{1,0:T(8,128)S(1)} custom-call(f32[128,128]{1,0:T(8,128)S(1)} %cholesky.604), custom_call_target="Cholesky" | custom-call | tf_op jit(solution)/shard_map/jit(cholesky)/cholesky | solution.py:22
  525.6 12.1 %cholesky.546 = f32[128,128]{1,0:T(8,128)S(1)} custom-call(f32[128,128]{1,0:T(8,128)S(1)} %cholesky.609), custom_call_target="Cholesky" | custom-call | tf_op jit(solution)/shard_map/jit(cholesky)/cholesky | solution.py:22
  551.5 11.7 %cholesky.564 = f32[128,128]{1,0:T(8,128)S(1)} custom-call(f32[128,128]{1,0:T(8,128)S(1)} %convolution_subtract_fusion.11), custom_call_target="Cholesky" | custom-call | tf_op jit(solution)/shard_map/jit(cholesky)/cholesky | solution.py:22
  581.4 23.4 %while.1 = (s32[]{:T(128)}, f32[1024,1024]{1,0:T(8,128)}, s32[8,2]{0,1:T(2,128)S(1)}, f32[8,128,128]{2,1,0:T(8,128)S(1)}, s32[]{:T(128)}) while((s32[]{:T(128)}, f32[1024,1024]{1,0:T(8,128)}, s32[8,2]{0,1:T(2,128)S(1)}, f32[8,128,128]{2,1,0:T(8,128)S(1)}, s32[]{:T(128)}) %tuple.74), condition=%wide.while_cond, body=%wide.while_body.sunk | while | flops 2 | bytes 131189 | solution.py:26
  604.8 78.8 %custom-call.70 = f32[8,128,128]{1,2,0:T(8,128)S(1)} custom-call(f32[8,128,128]{2,1,0:T(8,128)S(1)} %get-tuple-element.9), custom_call_target="InvertDiagBlocksLowerTriangular" | custom-call | tf_op jit(solution)/shard_map/jit(_solve_triangular)/triangular_solve | solution.py:26
  746.5 9.8 %convolution_subtract_fusion = f32[128,4096]{1,0:T(8,128)S(1)} fusion(f32[768,4096]{1,0:T(8,128)} %get-tuple-element.41, f32[1024,4096]{1,0:T(8,128)S(1)} %bitcast.131, f32[1024,1024]{1,0:T(8,128)} %get-tuple-element.146), kind=kOutput, calls=%fused_computation.26 | convolution fusion | flops 4832362496 | bytes 17170432 | tf_op jit(solution)/shard_map/jit(_solve_triangular)/triangular_solve | solution.py:26
  761.1 11.7 %convolution_subtract_fusion.4 = f32[128,4096]{1,0:T(8,128)S(1)} fusion(f32[896,4096]{1,0:T(8,128)} %get-tuple-element.37, f32[1024,4096]{1,0:T(8,128)S(1)} %bitcast.131, f32[1024,1024]{1,0:T(8,128)} %get-tuple-element.146), kind=kOutput, calls=%fused_computation.30 | convolution fusion | flops 5637668864 | bytes 19333120 | tf_op jit(solution)/shard_map/jit(_solve_triangular)/triangular_solve | solution.py:26
  786.2 11.9 %copy.27 = bf16[4096,1024]{1,0:T(8,128)(2,1)} copy(bf16[4096,1024]{0,1:T(8,128)(2,1)} %fusion) | data formatting | bytes 16777216
  (124 shorter events, 219.4 us)
Async XLA Ops:
  16.0 55.5 %all-to-all-start = ((bf16[8,128,1024]{2,1,0:T(8,128)(2,1)}), bf16[8,128,1024]{2,1,0:T(8,128)(2,1)S(1)}, u32[]{:S(2)}, u32[]{:S(2)}) async-start(bf16[8,128,1024]{2,1,0:T(8,128)(2,1)} %broadcast_select_fusion), calls=%async_computation | async-start | bytes 4194304 | tf_op jit(solution)/shard_map/all_to_all | solution.py:66
  23.3 243.3 %all-reduce.4.cloned.1.call-start = ((), (), s32[]{:S(2)}) async-start(), calls=%async_computation.1 | async-start | bytes 8388608 | tf_op jit(solution)/shard_map/psum | solution.py:15
  111.1 242.4 %all-reduce.6.cloned.1.call-start = ((), (), s32[]{:S(2)}) async-start(), calls=%async_computation.2 | async-start | bytes 8388608 | tf_op jit(solution)/shard_map/psum | solution.py:15
  363.5 1.9 copy-start
  683.6 29.7 %copy-start.1 = (f32[8,128,128]{1,2,0:T(8,128)}, f32[8,128,128]{1,2,0:T(8,128)S(1)}, u32[]{:S(2)}) copy-start(f32[8,128,128]{1,2,0:T(8,128)S(1)} %custom-call.70) | copy-start | bytes 1572868
  683.6 15.6 %slice-start = ((s8[16777216]{0:T(1024)(128)(4,1)}), s8[4194304]{0:T(1024)(128)(4,1)S(1)}, s32[]{:S(2)}) async-start(s8[16777216]{0:T(1024)(128)(4,1)} %bitcast.130), calls=%async_computation.3 | async-start | bytes 8388608
  683.6 15.6 %slice-start.1 = ((s8[16777216]{0:T(1024)(128)(4,1)}), s8[4194304]{0:T(1024)(128)(4,1)S(1)}, s32[]{:S(2)}) async-start(s8[16777216]{0:T(1024)(128)(4,1)} %bitcast.130), calls=%async_computation.4 | async-start | bytes 8388608
  689.7 9.5 %slice-start.2 = ((s8[16777216]{0:T(1024)(128)(4,1)}), s8[4194304]{0:T(1024)(128)(4,1)S(1)}, s32[]{:S(2)}) async-start(s8[16777216]{0:T(1024)(128)(4,1)} %bitcast.130), calls=%async_computation.5 | async-start | bytes 8388608
  693.5 5.8 slice-start.3
Sparse Core Ops, SparseCore 0:
  111.2 155.3 all-reduce.3
  269.0 84.4 all-reduce.5
